TPU v7x, 32 devices: a whole 2x2x4 slice. The times are simulated.
32 devices in a mesh: groups: 2 (over y), hist: 4 (over z), tower: 2 (over x), head: 2 (over core).
Axes of the slice: x: 2, y: 2, z: 4, core: 2. Of those that a mesh axis runs over, the one named last changes fastest.
Arguments:
- queries: bfloat16 [1024, 1024], P(('groups', 'hist', 'tower'), 'head'), parts along dimension 0, may hold values from -6 to 6
- hist_keys: bfloat16 [4, 1024, 1024], P('groups', 'hist', 'head'), parts along dimension 0, may hold values from -6 to 6
- hist_values: bfloat16 [4, 1024, 1024], P('groups', 'hist', 'head'), parts along dimension 0, may hold values from -6 to 6
- cand_user: int32 [1024], P(('groups', 'hist', 'tower')), parts along dimension 0, may hold values from 0 to 1
- time_bucket: int32 [4, 1024], P('groups', 'hist'), parts along dimension 0, may hold values from 0 to 127
- hist_len: int32 [4], P('groups'), parts along dimension 0, may hold values from 256 to 1024
- cand_gate: bfloat16 [1024, 1024], P(('groups', 'hist', 'tower'), 'head'), parts along dimension 0, may hold values from -6 to 6
- time_bias: float32 [128, 8], P(None, 'head'), may hold values from -4 to 4
- tower_in: bfloat16 [1024, 4096], P('head', 'tower'), may hold values from -0.1875 to 0.1875
- tower_bias: float32 [4096], P('tower'), may hold values from -4 to 4
- tower_out: float32 [4096], P('tower'), may hold values from -0.09375 to 0.09375
Outputs:
- cand_states: bfloat16 [1024, 1024], P(('groups', 'hist', 'tower'), 'head'), parts along dimension 0
- cand_scores: float32 [1024], P(('groups', 'hist', 'tower')), parts along dimension 0
There are 2 independent parts, one for each index of `groups`. A program takes and returns all parts, laid end to end along the dimension named above; an argument that names none is the same for every part. Nothing has to cross between parts.
All inputs are finite; a program needn't handle non-finite values.
Results may differ from a plain program's by a relative error of at most 0.017.
Values may be sent and summed in bfloat16 or wider, within the bound.
A program may use at most 64 MiB of HBM per device.

v0:
```python
import jax
import jax.numpy as jnp
from jax import lax
from jax.sharding import PartitionSpec as P

D = 1024
DH = 128


def local(
    queries,
    hist_keys,
    hist_values,
    cand_user,
    time_bucket,
    hist_len,
    cand_gate,
    time_bias,
    tower_in,
    tower_bias,
    tower_out,
):
    score_scale = DH ** (-0.5)
    user_count, per_user, feat_width = hist_keys.shape
    events = user_count * per_user
    key_rows = hist_keys.reshape(events, feat_width)
    value_rows = hist_values.reshape(events, feat_width)
    event_index = jnp.arange(events, dtype=jnp.int32)
    key_user = event_index // per_user
    position = lax.axis_index("hist") * per_user + event_index % per_user
    user_ids = jnp.arange(user_count, dtype=jnp.int32)
    lengths = jnp.sum(
        jnp.where(key_user[:, None] == user_ids[None, :], hist_len[None, :], 0), axis=1
    )
    key_live = position < lengths
    buckets = time_bucket.reshape(events)
    bucket_count = time_bias.shape[0]
    onehot = jnp.where(
        buckets[:, None] == jnp.arange(bucket_count, dtype=jnp.int32)[None, :], 1.0, 0.0
    ).astype(jnp.float32)
    key_bias = jnp.dot(onehot, time_bias, precision=lax.Precision.HIGHEST)
    query_all, user_all = (
        lax.all_gather(queries, "hist", axis=0, tiled=True),
        lax.all_gather(cand_user, "hist", axis=0, tiled=True),
    )
    same_user = jnp.where(
        (user_all[:, None] == key_user[None, :]) & key_live[None, :], 1.0, 0.0
    ).astype(jnp.float32)
    head_outputs = []
    for head_index in range(feat_width // DH):
        first = head_index * DH
        logits = lax.dot_general(
            query_all[:, first : first + DH],
            key_rows[:, first : first + DH],
            (((1,), (1,)), ((), ())),
            preferred_element_type=jnp.float32,
        )
        logits = logits * score_scale + key_bias[:, head_index][None, :]
        weights_bf = (jax.nn.silu(logits) * same_user).astype(jnp.bfloat16)
        head_outputs.append(
            jnp.dot(
                weights_bf, value_rows[:, first : first + DH], preferred_element_type=jnp.float32
            )
        )
    attended = lax.psum_scatter(
        jnp.concatenate(head_outputs, axis=1).astype(jnp.bfloat16),
        "hist",
        scatter_dimension=0,
        tiled=True,
    ).astype(jnp.float32)
    row_sum, row_squares = lax.psum(
        (jnp.sum(attended, axis=1), jnp.sum(attended * attended, axis=1)), "head"
    )
    row_mean = row_sum / D
    row_var = row_squares / D - row_mean * row_mean
    cand_states = (
        (attended - row_mean[:, None])
        * lax.rsqrt(row_var[:, None] + 1e-05)
        * cand_gate.astype(jnp.float32)
    ).astype(jnp.bfloat16)
    tower_rows = lax.all_gather(cand_states, "tower", axis=0, tiled=True)
    full_rows = lax.all_gather(tower_rows, "head", axis=1, tiled=True)
    full_weight = lax.all_gather(tower_in, "head", axis=0, tiled=True)
    pre_act = jnp.dot(full_rows, full_weight, preferred_element_type=jnp.float32)
    hidden = jax.nn.silu(pre_act + tower_bias[None, :])
    partial_scores = jnp.dot(hidden, tower_out, precision=lax.Precision.HIGHEST)
    cand_scores = lax.psum_scatter(partial_scores, "tower", scatter_dimension=0, tiled=True)
    return (cand_states, cand_scores)


def solution(mesh):
    return jax.shard_map(
        local,
        mesh=mesh,
        in_specs=(
            P(("groups", "hist", "tower"), "head"),
            P("groups", "hist", "head"),
            P("groups", "hist", "head"),
            P(("groups", "hist", "tower")),
            P("groups", "hist"),
            P("groups"),
            P(("groups", "hist", "tower"), "head"),
            P(None, "head"),
            P("head", "tower"),
            P("tower"),
            P("tower"),
        ),
        out_specs=(P(("groups", "hist", "tower"), "head"), P(("groups", "hist", "tower"))),
        check_vma=False,
    )
```

profile of v0, /device:TPU:0, one launch (start us, length us, event | category | flops | bytes accessed | tf_op | source)
XLA Modules:
  0.0 90.2 jit_solution(12852004160913523544)
XLA Ops:
  8.0 0.0 copy-start
  8.0 0.0 copy-start.5
  8.0 0.0 copy-start.4
  8.0 0.0 reduce-scatter.4.cloned.1.call-start
  8.1 1.3 %dynamic-slice = u32[1]{0:T(128)} dynamic-slice(u32[32]{0:T(128)} %constant.60, u32[]{:T(128)S(6)} %add.133), dynamic_slice_sizes={1} | dynamic-slice | bytes 12
  10.1 0.9 dynamic-update-slice
  10.9 9.9 %all-reduce = s32[256]{0:T(256)S(1)} all-reduce(s32[256]{0:T(256)S(1)} %dynamic-update-slice), channel_id=1, replica_groups=mesh['groups'=2,'hist'=4,'tower'=2,'head'=2] {'hist'}, use_global_device_ids=true, to_apply=%add | all-reduce | flops 256 | bytes 2048
  20.9 14.0 %all_gather.15 = bf16[256,512]{1,0:T(8,128)(2,1)S(1)} all-gather(bf16[64,512]{1,0:T(8,128)(2,1)} %param.11), channel_id=1, replica_groups=mesh['groups'=2,'hist'=4,'tower'=2,'head'=2] {'hist'}, dimensions={0}, use_global_device_ids=true | all-gather | bytes 327680 | tf_op jit(solution)/shard_map/all_gather | solution.py:43
  34.8 0.7 copy.23
  35.5 1.1 %fusion.34 = f32[512,4]{0,1:T(4,128)S(1)} fusion(f32[128,4]{0,1:T(4,128)} %param.18, s32[512]{0:T(512)S(1)} %bitcast.20), kind=kOutput, calls=%fused_computation.53 | convolution fusion | flops 3276800 | bytes 12288 | tf_op jit(solution)/shard_map/dot_general | solution.py:41
  36.6 0.7 fusion.71
  37.4 1.5 %convolution_convert_fusion.1 = bf16[256,128]{0,1:T(8,128)(2,1)S(1)} fusion(f32[512]{0:T(512)S(1)} %bitcast.24, s32[512]{0:T(512)S(1)} %add_select_fusion, s32[256]{0:T(256)S(1)} %all-reduce, pred[512]{0:T(512)(128)(4,1)S(1)} %fusion.77, bf16[512,512]{1,0:T(8,128)(2,1)} %bitcast.25, bf16[512,512]{1,0:T(8,128)(2,1)} %bitcast.29, ...), kind=kOutput, calls=%fused_computation.10 | convolution fusion | flops 68583424 | bytes 398848 | tf_op jit(solution)/shard_map/dot_general | solution.py:61
  38.9 1.5 %convolution_convert_fusion.2 = bf16[256,128]{0,1:T(8,128)(2,1)S(1)} fusion(f32[512]{0:T(512)S(1)} %bitcast.23, s32[512]{0:T(512)S(1)} %add_select_fusion, s32[256]{0:T(256)S(1)} %all-reduce, pred[512]{0:T(512)(128)(4,1)S(1)} %fusion.77, bf16[512,512]{1,0:T(8,128)(2,1)} %bitcast.26, bf16[512,512]{1,0:T(8,128)(2,1)} %bitcast.30, ...), kind=kOutput, calls=%fused_computation.11 | convolution fusion | flops 68583424 | bytes 398848 | tf_op jit(solution)/shard_map/dot_general | solution.py:61
  40.4 0.0 copy-done.5
  40.4 0.0 copy-done.4
  40.5 0.5 convolution_convert_fusion.3
  41.0 0.0 copy-start.2
  41.0 0.0 copy-start.6
  41.0 0.0 copy-start.3
  41.0 0.5 convolution_convert_fusion
  41.6 0.8 copy.21
  42.4 0.0 reduce-scatter.4.cloned.1.call-update
  42.5 0.0 all-gather.2.cloned.1.call-start
  42.5 0.5 all-gather.2.cloned.1.call-update
  43.1 0.0 copy-done.2
  43.1 0.1 copy.18
  43.2 0.0 copy-done.6
  43.2 0.6 dynamic-slice.1
  44.4 18.1 %reduce-scatter.4.cloned.1.call-done = bf16[64,512]{1,0:T(8,128)(2,1)} async-done(((bf16[256,512]{1,0:T(8,128)(2,1)}), bf16[64,512]{1,0:T(8,128)(2,1)}) %reduce-scatter.4.cloned.1.call-update) | async-done | bytes 65552
  62.6 1.0 %copy.22 = bf16[64,512]{0,1:T(8,128)(2,1)S(1)} copy(bf16[64,512]{1,0:T(8,128)(2,1)} %reduce-scatter.4.cloned.1.call-done) | data formatting | bytes 131072
  63.5 0.1 convert_reduce_fusion
  63.6 2.5 %all-reduce.2 = (f32[64]{0:T(128)S(1)}, f32[64]{0:T(128)S(1)}) all-reduce(f32[64]{0:T(128)S(1)} %get-tuple-element.9, f32[64]{0:T(128)S(1)} %get-tuple-element.8), channel_id=1, replica_groups=mesh['groups'=2,'hist'=4,'tower'=2,'head'=2] {'head'}, use_global_device_ids=true, to_apply=%region_5.6 | all-reduce | flops 128 | bytes 1024 | tf_op jit(solution)/shard_map/psum | solution.py:71
  66.1 0.1 fusion.16
  66.2 0.1 copy.20
  66.3 0.0 copy-start.1
  66.3 4.9 %all_gather.17 = bf16[128,512]{1,0:T(8,128)(2,1)S(1)} all-gather(bf16[64,512]{1,0:T(8,128)(2,1)S(1)} %copy.20), channel_id=1, replica_groups=mesh['groups'=2,'hist'=4,'tower'=2,'head'=2] {'tower'}, dimensions={0}, use_global_device_ids=true | all-gather | bytes 196608 | tf_op jit(solution)/shard_map/all_gather | solution.py:81
  71.2 2.0 %all_gather.18 = bf16[128,1024]{1,0:T(8,128)(2,1)S(1)} all-gather(bf16[128,512]{1,0:T(8,128)(2,1)S(1)} %all_gather.17), channel_id=1, replica_groups=mesh['groups'=2,'hist'=4,'tower'=2,'head'=2] {'head'}, dimensions={1}, use_global_device_ids=true | all-gather | bytes 393216 | tf_op jit(solution)/shard_map/all_gather | solution.py:82
  73.2 0.0 all-gather.2.cloned.1.call-done
  73.2 0.0 copy-done.3
  73.2 2.9 %convolution_add_fusion = f32[128,2048]{1,0:T(8,128)S(1)} fusion(bf16[128,1024]{1,0:T(8,128)(2,1)S(1)} %all_gather.18, bf16[1024,2048]{1,0:T(8,128)(2,1)} %all-gather.2.cloned.1.call-done, f32[2048]{0:T(1024)S(1)} %copy-done.3), kind=kOutput, calls=%fused_computation | convolution fusion | flops 537133056 | bytes 5513216 | tf_op jit(solution)/shard_map/dot_general | solution.py:84
  76.1 0.0 copy-done
  76.2 1.1 %convolution_bitcast_fusion = f32[128]{0:T(128)S(1)} fusion(f32[2048,1]{0,1:T(1,128)S(1)} %bitcast.18, f32[128,2048]{1,0:T(8,128)S(1)} %convolution_add_fusion), kind=kOutput, calls=%fused_computation.13 | convolution fusion | flops 4194304 | bytes 1057280 | tf_op jit(solution)/shard_map/dot_general | solution.py:86
  77.2 0.0 copy-done.1
  77.2 4.9 %all-reduce.1 = f32[128]{0:T(128)S(1)} all-reduce(f32[128]{0:T(128)S(1)} %convolution_bitcast_fusion), channel_id=3, replica_groups=mesh['groups'=2,'hist'=4,'tower'=2,'head'=2] {'tower'}, use_global_device_ids=true, to_apply=%region_6.7.clone | all-reduce | flops 128 | bytes 1024
  82.2 0.6 dynamic-slice.2
  (6 shorter events, 0.1 us)
Async XLA Ops:
  8.0 68.2 %copy-start = (f32[2048]{0:T(1024)S(1)}, f32[2048]{0:T(1024)}, u32[]{:S(2)}) copy-start(f32[2048]{0:T(1024)} %param.21) | copy-start | bytes 24580
  8.0 32.4 %copy-start.5 = (bf16[2,256,512]{2,1,0:T(8,128)(2,1)S(1)}, bf16[2,256,512]{2,1,0:T(8,128)(2,1)}, u32[]{:S(2)}) copy-start(bf16[2,256,512]{2,1,0:T(8,128)(2,1)} %param.12) | copy-start | bytes 1572868
  8.0 32.4 %copy-start.4 = (bf16[2,256,512]{2,1,0:T(8,128)(2,1)S(1)}, bf16[2,256,512]{2,1,0:T(8,128)(2,1)}, u32[]{:S(2)}) copy-start(bf16[2,256,512]{2,1,0:T(8,128)(2,1)} %param.13) | copy-start | bytes 1572868
  8.0 54.5 %reduce-scatter.4.cloned.1.call-start = ((), (), s32[]{:S(2)}) async-start(), calls=%async_computation.2 | async-start | bytes 327680
  41.0 2.1 %copy-start.2 = (bf16[64,512]{1,0:T(8,128)(2,1)S(1)}, bf16[64,512]{1,0:T(8,128)(2,1)}, u32[]{:S(2)}) copy-start(bf16[64,512]{1,0:T(8,128)(2,1)} %param.17) | copy-start | bytes 196612
  41.0 2.2 %copy-start.6 = (u32[32]{0:T(128)S(1)}, u32[32]{0:T(128)}, u32[]{:S(2)}) copy-start(u32[32]{0:T(128)} %constant.66) | copy-start | bytes 388
  41.0 32.2 %copy-start.3 = (f32[2048]{0:T(1024)S(1)}, f32[2048]{0:T(1024)}, u32[]{:S(2)}) copy-start(f32[2048]{0:T(1024)} %param.20) | copy-start | bytes 24580
  42.5 30.7 %all-gather.2.cloned.1.call-start = ((), (), s32[]{:S(2)}) async-start(), calls=%async_computation.1 | async-start | bytes 6291456 | tf_op jit(solution)/shard_map/all_gather | solution.py:83
  66.3 11.0 %copy-start.1 = (bf16[64,512]{1,0:T(8,128)(2,1)}, bf16[64,512]{1,0:T(8,128)(2,1)S(1)}, u32[]{:S(2)}) copy-start(bf16[64,512]{1,0:T(8,128)(2,1)S(1)} %copy.20) | copy-start | bytes 196612
Sparse Core Ops, SparseCore 0:
  42.6 19.9 reduce-scatter.3
Sparse Core Ops, SparseCore 1:
  44.5 13.5 all-gather.1
where the time goes:
time: 90.6 us; the launch traced here: 90.2 us
  blocking collectives  38.2 us (42%)
  waiting for transfers between devices  18.7 us (21%)
  between operations  17 us (19%)
  matrix products  9.22 us (10%)
  local copies, waits for them, and re-layouts  6.1 us (7%)
  other arithmetic  0.93 us (1%)
    unnamed x3, waiting for transfers between devices  18.7 us
    unnamed x2, blocking collectives  14.8 us
    all_gather x1, blocking collectives, local(): lax.all_gather(queries, 'hist', axis=0, tiled=True)  14 us
    unnamed x24, local copies, waits for them, and re-layouts  6.08 us
    all_gather x1, blocking collectives, local(): tower_rows = lax.all_gather(cand_states, 'tower', axis=0, tiled=True)  4.93 us
    dot_general x4, matrix products, local(): jnp.dot(weights_bf, value_rows[:, first:first + DH], preferred_element_ty...  4.12 us
    dot_general x1, matrix products, local(): jnp.dot(full_rows, full_weight, preferred_element_type=jnp.float32)  2.92 us
    psum x1, blocking collectives, local(): lax.psum((jnp.sum(attended, axis=1), jnp.sum(attended * attended, axis=1)...  2.47 us
  transfers between devices with their start and end apart: 2, of which 1 were waited for; matrix products, arithmetic and copies ran while one was open for 2% of the time, Pallas kernels for 0%

commit v1 on v0

v1 whole, which is shorter than its diff:
```python
import functools

import jax
import jax.numpy as jnp
from jax import lax
from jax.experimental import pallas as pl
from jax.experimental.pallas import tpu as pltpu
from jax.sharding import PartitionSpec as P

DH = 128
MESH = pl.DeviceIdType.MESH
F32 = jnp.float32
BF16 = jnp.bfloat16


def partner_of(me, step, count):
    if count & (count - 1):
        return lax.rem(me + step, count)
    other, bit = 0, 1
    while bit < count:
        mine = lax.rem(me // bit, 2)
        other = other + (1 - mine if step & bit else mine) * bit
        bit *= 2
    return other


def source_of(me, step, count):
    if count & (count - 1):
        return lax.rem(me + count - step, count)
    return partner_of(me, step, count)


def kernel(
    n_hist,
    n_tower,
    q_hbm,
    k_hbm,
    v_hbm,
    user_hbm,
    bucket_hbm,
    len_ref,
    gate_hbm,
    tbias_hbm,
    w_hbm,
    b_hbm,
    o_hbm,
    states_out,
    scores_out,
    q_all,
    u_all,
    k_buf,
    v_buf,
    bucket,
    gate,
    tbias,
    w_buf,
    b_buf,
    o_buf,
    share_out,
    share_in,
    stat_buf,
    state_buf,
    score_send,
    score_in,
    load_sem,
    q_send,
    q_recv,
    u_send,
    u_recv,
    share_send,
    share_recv,
    one_send,
    one_recv,
    state_send,
    state_recv,
    score_send_sem,
    score_recv,
):
    z = lax.axis_index("hist")
    x = lax.axis_index("tower")
    c = lax.axis_index("head")
    mate = 1 - c
    rows, feat = q_hbm.shape
    users, per_user, _ = k_hbm.shape
    hidden = b_buf.shape[1]
    total_feat = 2 * feat

    tower_peers = [(t, h) for t in range(n_tower) for h in range(2) if t or h]

    def tower_id(t, h):
        return {"tower": partner_of(x, t, n_tower), "head": mate if h else c}

    barrier = pltpu.get_barrier_semaphore()
    for step in range(1, n_hist):
        pl.semaphore_signal(
            barrier, inc=1, device_id={"hist": partner_of(z, step, n_hist)}, device_id_type=MESH
        )
    for t, h in tower_peers:
        pl.semaphore_signal(barrier, inc=1, device_id=tower_id(t, h), device_id_type=MESH)

    mine_cols = pl.ds(pl.multiple_of(c * hidden, 128), hidden)
    mate_cols = pl.ds(pl.multiple_of(mate * hidden, 128), hidden)
    loads = [
        pltpu.make_async_copy(src, dst, load_sem.at[i])
        for i, (src, dst) in enumerate(
            [
                (q_hbm, q_all.at[z]),
                (user_hbm, u_all.at[z]),
                (bucket_hbm, bucket),
                (tbias_hbm, tbias),
                (k_hbm, k_buf),
                (v_hbm, v_buf),
                (gate_hbm, gate),
                (b_hbm.at[:, mine_cols], b_buf),
                (o_hbm.at[:, mine_cols], o_buf),
                (w_hbm.at[:, mine_cols], w_buf.at[c]),
            ]
        )
    ]
    for load in loads:
        load.start()

    pl.semaphore_wait(barrier, n_hist - 1 + len(tower_peers))

    def remote(src, dst, send, recv, device_id):
        return pltpu.make_async_remote_copy(
            src_ref=src,
            dst_ref=dst,
            send_sem=send,
            recv_sem=recv,
            device_id=device_id,
            device_id_type=MESH,
        )

    sends = []
    order = list(range(2, n_hist)) + [1] if n_hist > 1 else []
    for step in order:
        to = {"hist": partner_of(z, step, n_hist)}
        u_copy = remote(user_hbm, u_all.at[z], u_send.at[step], u_recv.at[z], to)
        u_copy.start()
        q_copy = remote(q_hbm, q_all.at[z], q_send.at[step], q_recv.at[z], to)
        q_copy.start()
        sends += [u_copy, q_copy]
    w_copy = remote(
        w_hbm.at[:, mate_cols], w_buf.at[c], one_send.at[0], one_recv.at[0], {"head": mate}
    )
    w_copy.start()
    sends.append(w_copy)

    loads[2].wait()
    loads[3].wait()
    bucket_count, heads = tbias.shape
    half_scale = 0.5 * DH ** (-0.5)
    tb = tbias[...] * 0.5
    bias_rows, owner_rows = [], []
    for u in range(users):
        onehot = jnp.where(
            lax.broadcasted_iota(jnp.int32, (bucket_count, per_user), 0) == bucket[u : u + 1, :],
            1.0,
            0.0,
        ).astype(F32)
        bias_rows.append(
            lax.dot_general(
                tb,
                onehot,
                (((0,), (0,)), ((), ())),
                precision=lax.Precision.HIGHEST,
                preferred_element_type=F32,
            )
        )
        position = z * per_user + lax.broadcasted_iota(jnp.int32, (1, per_user), 1)
        owner_rows.append(jnp.where(position < len_ref[u], u, -1))
    bias = jnp.concatenate(bias_rows, axis=1)
    owner = jnp.concatenate(owner_rows, axis=1)
    events = users * per_user

    loads[0].wait()
    loads[1].wait()
    loads[4].wait()
    loads[5].wait()

    def attend(index, out_ref):
        user_col = jnp.broadcast_to(u_all[index], (128, rows)).T[:, :1]
        live = jnp.where(user_col == owner, 1.0, 0.0).astype(F32)
        for head in range(heads):
            cols = slice(head * DH, (head + 1) * DH)
            s = lax.dot_general(
                q_all[index, :, cols],
                k_buf[:, :, cols].reshape(events, DH),
                (((1,), (1,)), ((), ())),
                preferred_element_type=F32,
            )
            half = s * half_scale + bias[head : head + 1, :]
            weight = ((half + half * jnp.tanh(half)) * live).astype(BF16)
            out_ref[:, cols] = jnp.dot(
                weight, v_buf[:, :, cols].reshape(events, DH), preferred_element_type=F32
            ).astype(BF16)

    attend(z, share_in.at[z])
    for step in range(1, n_hist):
        src = source_of(z, step, n_hist)
        remote(user_hbm, u_all.at[src], u_send.at[step], u_recv.at[src], {"hist": src}).wait_recv()
        remote(q_hbm, q_all.at[src], q_send.at[step], q_recv.at[src], {"hist": src}).wait_recv()
        attend(src, share_out.at[step])
        copy = remote(
            share_out.at[step],
            share_in.at[z],
            share_send.at[step],
            share_recv.at[z],
            {"hist": src},
        )
        copy.start()
        sends.append(copy)

    for step in range(1, n_hist):
        src = partner_of(z, step, n_hist)
        remote(
            share_out.at[step], share_in.at[src], share_send.at[step], share_recv.at[src], {"hist": src}
        ).wait_recv()
    attended = share_in[0].astype(F32)
    for s in range(1, n_hist):
        attended = attended + share_in[s].astype(F32)

    row_sum = jnp.sum(attended, axis=1, keepdims=True)
    row_squares = jnp.sum(attended * attended, axis=1, keepdims=True)
    lane = lax.broadcasted_iota(jnp.int32, (rows, 128), 1)
    stat_buf[c] = jnp.where(lane == 0, row_sum, row_squares)
    stat_copy = remote(
        stat_buf.at[c], stat_buf.at[c], one_send.at[1], one_recv.at[1], {"head": mate}
    )
    stat_copy.start()
    sends.append(stat_copy)
    loads[6].wait()
    remote(
        stat_buf.at[mate], stat_buf.at[mate], one_send.at[1], one_recv.at[1], {"head": mate}
    ).wait_recv()
    stats = stat_buf[0] + stat_buf[1]
    row_mean = stats[:, 0:1] / total_feat
    row_var = stats[:, 1:2] / total_feat - row_mean * row_mean
    state_buf[x, c] = (
        (attended - row_mean) * lax.rsqrt(row_var + 1e-05) * gate[...].astype(F32)
    ).astype(BF16)

    for i, (t, h) in enumerate(tower_peers):
        copy = remote(
            state_buf.at[x, c],
            state_buf.at[x, c],
            state_send.at[i],
            state_recv.at[x, c],
            tower_id(t, h),
        )
        copy.start()
        sends.append(copy)
    states_out[...] = state_buf[x, c]

    loads[7].wait()
    loads[8].wait()
    loads[9].wait()
    remote(
        w_hbm.at[:, mate_cols], w_buf.at[mate], one_send.at[0], one_recv.at[0], {"head": mate}
    ).wait_recv()

    def wait_state(tower, head):
        remote(
            state_buf.at[tower, head],
            state_buf.at[tower, head],
            state_send.at[0],
            state_recv.at[tower, head],
            {"head": mate},
        ).wait_recv()

    def tower_scores(tower):
        pre = jnp.dot(state_buf[tower, 0], w_buf[0], preferred_element_type=F32)
        pre = pre + jnp.dot(state_buf[tower, 1], w_buf[1], preferred_element_type=F32)
        half = (pre + b_buf[...]) * 0.5
        part = (half + half * jnp.tanh(half)) * o_buf[...]
        acc = part[:, 0:128]
        for i in range(1, hidden // 128):
            acc = acc + part[:, i * 128 : (i + 1) * 128]
        return jnp.broadcast_to(jnp.sum(acc.T, axis=0, keepdims=True), (8, rows))

    wait_state(x, mate)
    own_scores = tower_scores(x)
    score_in[x, c] = own_scores
    copy = remote(
        score_in.at[x, c], score_in.at[x, c], score_send_sem.at[0], score_recv.at[x, c], {"head": mate}
    )
    copy.start()
    sends.append(copy)
    for t in range(1, n_tower):
        other = source_of(x, t, n_tower)
        wait_state(other, c)
        wait_state(other, mate)
        score_send[t] = tower_scores(other)
        for h in range(2):
            copy = remote(
                score_send.at[t],
                score_in.at[x, c],
                score_send_sem.at[2 * t + h],
                score_recv.at[x, c],
                {"tower": other, "head": mate if h else c},
            )
            copy.start()
            sends.append(copy)

    for t, h in tower_peers:
        tower, head = partner_of(x, t, n_tower), mate if h else c
        remote(
            score_in.at[tower, head],
            score_in.at[tower, head],
            score_send_sem.at[0],
            score_recv.at[tower, head],
            {"head": mate},
        ).wait_recv()
    total = score_in[0, 0] + score_in[0, 1]
    for t in range(1, n_tower):
        total = total + (score_in[t, 0] + score_in[t, 1])
    scores_out[...] = total[0:1, :]
    for copy in sends:
        copy.wait_send()


def local(
    queries,
    hist_keys,
    hist_values,
    cand_user,
    time_bucket,
    hist_len,
    cand_gate,
    time_bias,
    tower_in,
    tower_bias,
    tower_out,
    *,
    n_hist,
    n_tower,
):
    rows, feat = queries.shape
    hidden = tower_in.shape[1] // 2
    any_spec = pl.BlockSpec(memory_space=pl.ANY)
    vmem_spec = pl.BlockSpec(memory_space=pltpu.VMEM)
    dma = pltpu.SemaphoreType.DMA
    states, scores = pl.pallas_call(
        functools.partial(kernel, n_hist, n_tower),
        out_shape=(
            jax.ShapeDtypeStruct((rows, feat), BF16),
            jax.ShapeDtypeStruct((1, rows), F32),
        ),
        in_specs=[any_spec] * 5 + [pl.BlockSpec(memory_space=pltpu.SMEM)] + [any_spec] * 5,
        out_specs=(vmem_spec, vmem_spec),
        scratch_shapes=[
            pltpu.VMEM((n_hist, rows, feat), BF16),
            pltpu.VMEM((n_hist, 1, rows), jnp.int32),
            pltpu.VMEM(hist_keys.shape, BF16),
            pltpu.VMEM(hist_values.shape, BF16),
            pltpu.VMEM(time_bucket.shape, jnp.int32),
            pltpu.VMEM((rows, feat), BF16),
            pltpu.VMEM(time_bias.shape, F32),
            pltpu.VMEM((2, feat, hidden), BF16),
            pltpu.VMEM((1, hidden), F32),
            pltpu.VMEM((1, hidden), F32),
            pltpu.VMEM((n_hist, rows, feat), BF16),
            pltpu.VMEM((n_hist, rows, feat), BF16),
            pltpu.VMEM((2, rows, 128), F32),
            pltpu.VMEM((n_tower, 2, rows, feat), BF16),
            pltpu.VMEM((n_tower, 8, rows), F32),
            pltpu.VMEM((n_tower, 2, 8, rows), F32),
            dma((10,)),
            dma((n_hist,)),
            dma((n_hist,)),
            dma((n_hist,)),
            dma((n_hist,)),
            dma((n_hist,)),
            dma((n_hist,)),
            dma((2,)),
            dma((2,)),
            dma((2 * n_tower,)),
            dma((n_tower, 2)),
            dma((2 * n_tower,)),
            dma((n_tower, 2)),
        ],
        compiler_params=pltpu.CompilerParams(collective_id=0, has_side_effects=True),
    )(
        queries,
        hist_keys,
        hist_values,
        cand_user.reshape(1, rows),
        time_bucket,
        hist_len,
        cand_gate,
        time_bias,
        tower_in,
        tower_bias.reshape(1, -1),
        tower_out.reshape(1, -1),
    )
    return states, scores.reshape(rows)


def solution(mesh):
    return jax.shard_map(
        functools.partial(local, n_hist=mesh.shape["hist"], n_tower=mesh.shape["tower"]),
        mesh=mesh,
        in_specs=(
            P(("groups", "hist", "tower"), "head"),
            P("groups", "hist", "head"),
            P("groups", "hist", "head"),
            P(("groups", "hist", "tower")),
            P("groups", "hist"),
            P("groups"),
            P(("groups", "hist", "tower"), "head"),
            P(None, "head"),
            P("head", "tower"),
            P("tower"),
            P("tower"),
        ),
        out_specs=(P(("groups", "hist", "tower"), "head"), P(("groups", "hist", "tower"))),
        check_vma=False,
    )
```

time: 90.6 us -> 34 us (0.38)
  blocking collectives: 38.2 us -> 0 us
  Pallas kernels: 0 us -> 29.1 us
  waiting for transfers between devices: 18.7 us -> 0 us
  between operations: 17 us -> 0.64 us
  matrix products: 9.22 us -> 0 us
  local copies, waits for them, and re-layouts: 6.1 us -> 4.01 us
  other arithmetic: 0.93 us -> 0 us
    pallas_call x0 -> x1, Pallas kernels: none -> 29.1 us  [local(): pl.pallas_call(functools.partial(kernel, n_hist, n_tower), out_shape=(jax...]
    all_gather x3 -> x0, blocking collectives: 20.9 us -> none  [the longest x1 14 us: local(): lax.all_gather(queries, 'hist', axis=0, tiled=True)]
    unnamed x3 -> x0, waiting for transfers between devices: 18.7 us -> none
    unnamed x2 -> x0, blocking collectives: 14.8 us -> none
    dot_general x7 -> x0, matrix products: 9.22 us -> none  [the longest x4 4.12 us: local(): jnp.dot(weights_bf, value_rows[:, first:first + DH], preferred_element_ty...]
    psum x1 -> x0, blocking collectives: 2.47 us -> none  [local(): lax.psum((jnp.sum(attended, axis=1), jnp.sum(attended * attended, axis=1)...]
    unnamed x24 -> x3, local copies, waits for them, and re-layouts: 6.08 us -> 4.01 us
  transfers between devices with their start and end apart: 2 -> 0, of which waited for: 1 -> 0; matrix products, arithmetic and copies ran while one was open for 2% -> 0% of each run, Pallas kernels for 0% -> 0%
where the time goes in v1:
time: 34 us; the launch traced here: 33.8 us
  Pallas kernels  29.1 us (86%)
  local copies, waits for them, and re-layouts  4.01 us (12%)
  between operations  0.64 us (2%)
    pallas_call x1, Pallas kernels, local(): pl.pallas_call(functools.partial(kernel, n_hist, n_tower), out_shape=(jax...  29.1 us
    unnamed x3, local copies, waits for them, and re-layouts  4.01 us

profile of v1, /device:TPU:0, one launch (start us, length us, event | category | flops | bytes accessed | tf_op | source)
XLA Modules:
  0.0 33.8 jit_solution(10194173290597118499)
XLA Ops:
  0.6 1.4 %copy.13.tbias_hbm = f32[128,4]{1,0:T(8,128)} copy(f32[128,4]{0,1:T(4,128)} %param.18) | data formatting | bytes 4096 | tf_op args[7]
  2.0 29.1 %shard_map.122 = (bf16[64,512]{1,0:T(8,128)(2,1)}, f32[1,64]{1,0:T(1,128)}) custom-call(bf16[64,512]{1,0:T(8,128)(2,1)} %q_hbm.1, bf16[2,256,512]{2,1,0:T(8,128)(2,1)} %k_hbm.1, bf16[2,256,512]{2,1,0:T(8,128)(2,1)} %v_hbm.1, s32[1,64]{1,0:T(1,128)} %bitcast.6, s32[2,256]{1,0:T(2,128)} %bucket_hbm.1, s32[2]{0:T(128)} %len_ref.1, bf16[64,512]{1,0:T(8,128)(2,1)} %gate_hbm.1, ...), custom_call_target="tpu_custom_call" | custom-call | tf_op jit(solution)/shard_map/pallas_call | solution.py:344
  31.2 1.5 %copy.16 = bf16[64,512]{1,0:T(8,128)(2,1)} copy(bf16[64,512]{1,0:T(8,128)(2,1)} %get-tuple-element.8) | data formatting | bytes 131072
  32.7 1.1 %copy.17 = f32[64]{0:T(128)} copy(f32[64]{0:T(128)} %bitcast.7) | data formatting | bytes 512

commit v2 on v1

--- a/solution.py
+++ b/solution.py
@@ -8,6 +8,7 @@
 from jax.sharding import PartitionSpec as P
 
 DH = 128
+CHUNKS = 2
 MESH = pl.DeviceIdType.MESH
 F32 = jnp.float32
 BF16 = jnp.bfloat16
@@ -46,6 +47,7 @@
     o_hbm,
     states_out,
     scores_out,
+    q_own,
     q_all,
     u_all,
     k_buf,
@@ -63,6 +65,7 @@
     score_send,
     score_in,
     load_sem,
+    ready,
     q_send,
     q_recv,
     u_send,
@@ -90,11 +93,16 @@
     def tower_id(t, h):
         return {"tower": partner_of(x, t, n_tower), "head": mate if h else c}
 
+    has_left, has_right = z > 0, z < n_hist - 1
+    sides = ((has_left, z - 1), (has_right, z + 1))
+
     barrier = pltpu.get_barrier_semaphore()
-    for step in range(1, n_hist):
-        pl.semaphore_signal(
-            barrier, inc=1, device_id={"hist": partner_of(z, step, n_hist)}, device_id_type=MESH
-        )
+    for exists, there in sides:
+
+        @pl.when(exists)
+        def _(there=there):
+            pl.semaphore_signal(barrier, inc=1, device_id={"hist": there}, device_id_type=MESH)
+
     for t, h in tower_peers:
         pl.semaphore_signal(barrier, inc=1, device_id=tower_id(t, h), device_id_type=MESH)
 
@@ -104,7 +112,7 @@
         pltpu.make_async_copy(src, dst, load_sem.at[i])
         for i, (src, dst) in enumerate(
             [
-                (q_hbm, q_all.at[z]),
+                (q_hbm, q_own),
                 (user_hbm, u_all.at[z]),
                 (bucket_hbm, bucket),
                 (tbias_hbm, tbias),
@@ -120,7 +128,8 @@
     for load in loads:
         load.start()
 
-    pl.semaphore_wait(barrier, n_hist - 1 + len(tower_peers))
+    neighbours = has_left.astype(jnp.int32) + has_right.astype(jnp.int32)
+    pl.semaphore_wait(barrier, neighbours + len(tower_peers))
 
     def remote(src, dst, send, recv, device_id):
         return pltpu.make_async_remote_copy(
@@ -132,15 +141,45 @@
             device_id_type=MESH,
         )
 
+    chunks = q_all.shape[1]
+    width = feat // chunks
+
+    def query_copy(there, chunk):
+        return remote(
+            q_hbm.at[:, chunk * width : (chunk + 1) * width],
+            q_all.at[z, chunk],
+            q_send.at[there, chunk],
+            q_recv.at[z, chunk],
+            {"hist": there},
+        )
+
+    def user_copy(there):
+        return remote(user_hbm, u_all.at[z], u_send.at[there], u_recv.at[z], {"hist": there})
+
+    def each_other(action):
+        for distance in range(1, n_hist):
+            for sign, behind in ((-1, has_right), (1, has_left)):
+                there = z + sign * distance
+                pl.when((there >= 0) & (there < n_hist))(
+                    functools.partial(action, distance, there, z - sign, behind)
+                )
+
+    def send_queries(distance, there, back, behind):
+        if distance > 1:
+            pl.semaphore_wait(ready.at[there], 1)
+
+        @pl.when(behind)
+        def _():
+            pl.semaphore_signal(
+                ready.at[there], inc=1, device_id={"hist": back}, device_id_type=MESH
+            )
+
+        user_copy(there).start()
+        for chunk in range(chunks):
+            query_copy(there, chunk).start()
+
+    each_other(send_queries)
     sends = []
-    order = list(range(2, n_hist)) + [1] if n_hist > 1 else []
-    for step in order:
-        to = {"hist": partner_of(z, step, n_hist)}
-        u_copy = remote(user_hbm, u_all.at[z], u_send.at[step], u_recv.at[z], to)
-        u_copy.start()
-        q_copy = remote(q_hbm, q_all.at[z], q_send.at[step], q_recv.at[z], to)
-        q_copy.start()
-        sends += [u_copy, q_copy]
     w_copy = remote(
         w_hbm.at[:, mate_cols], w_buf.at[c], one_send.at[0], one_recv.at[0], {"head": mate}
     )
@@ -149,7 +188,7 @@
 
     loads[2].wait()
     loads[3].wait()
-    bucket_count, heads = tbias.shape
+    heads, bucket_count = tbias.shape
     half_scale = 0.5 * DH ** (-0.5)
     tb = tbias[...] * 0.5
     bias_rows, owner_rows = [], []
@@ -163,7 +202,7 @@
             lax.dot_general(
                 tb,
                 onehot,
-                (((0,), (0,)), ((), ())),
+                (((1,), (0,)), ((), ())),
                 precision=lax.Precision.HIGHEST,
                 preferred_element_type=F32,
             )
@@ -179,47 +218,94 @@
     loads[4].wait()
     loads[5].wait()
 
-    def attend(index, out_ref):
+    def live_of(index):
         user_col = jnp.broadcast_to(u_all[index], (128, rows)).T[:, :1]
-        live = jnp.where(user_col == owner, 1.0, 0.0).astype(F32)
-        for head in range(heads):
-            cols = slice(head * DH, (head + 1) * DH)
-            s = lax.dot_general(
-                q_all[index, :, cols],
-                k_buf[:, :, cols].reshape(events, DH),
-                (((1,), (1,)), ((), ())),
-                preferred_element_type=F32,
-            )
-            half = s * half_scale + bias[head : head + 1, :]
-            weight = ((half + half * jnp.tanh(half)) * live).astype(BF16)
-            out_ref[:, cols] = jnp.dot(
-                weight, v_buf[:, :, cols].reshape(events, DH), preferred_element_type=F32
-            ).astype(BF16)
-
-    attend(z, share_in.at[z])
+        return jnp.where(user_col == owner, 1.0, 0.0).astype(F32)
+
+    def attend(query, live, head):
+        cols = slice(head * DH, (head + 1) * DH)
+        s = lax.dot_general(
+            query,
+            k_buf[:, :, cols].reshape(events, DH),
+            (((1,), (1,)), ((), ())),
+            preferred_element_type=F32,
+        )
+        half = s * half_scale + bias[head : head + 1, :]
+        weight = ((half + half * jnp.tanh(half)) * live).astype(BF16)
+        return jnp.dot(
+            weight, v_buf[:, :, cols].reshape(events, DH), preferred_element_type=F32
+        ).astype(BF16)
+
+    per_chunk = heads // chunks
+    own_live = live_of(z)
+    for head in range(heads):
+        cols = slice((head % per_chunk) * DH, (head % per_chunk + 1) * DH)
+        share_in[z, head // per_chunk, :, cols] = attend(
+            q_own[:, head * DH : (head + 1) * DH], own_live, head
+        )
+
+    nearer = jnp.minimum(z, n_hist - 1 - z)
+
+    def block_at(step):
+        distance = (step + 1) // 2
+        paired = z - distance if step % 2 else z + distance
+        rest = jnp.where(z < n_hist - 1 - z, z + step - nearer, z - step + nearer)
+        return jnp.where(step <= 2 * nearer, paired, rest)
+
+    def arrive(block, chunk):
+        if chunk == 0:
+            remote(
+                user_hbm, u_all.at[block], u_send.at[block], u_recv.at[block], {"hist": block}
+            ).wait_recv()
+        remote(
+            q_hbm.at[:, 0:width],
+            q_all.at[block, chunk],
+            q_send.at[block, chunk],
+            q_recv.at[block, chunk],
+            {"hist": block},
+        ).wait_recv()
+
+    def share_copy(step, chunk):
+        return remote(
+            share_out.at[step, chunk],
+            share_in.at[z, chunk],
+            share_send.at[step, chunk],
+            share_recv.at[z, chunk],
+            {"hist": block_at(step)},
+        )
+
     for step in range(1, n_hist):
-        src = source_of(z, step, n_hist)
-        remote(user_hbm, u_all.at[src], u_send.at[step], u_recv.at[src], {"hist": src}).wait_recv()
-        remote(q_hbm, q_all.at[src], q_send.at[step], q_recv.at[src], {"hist": src}).wait_recv()
-        attend(src, share_out.at[step])
-        copy = remote(
-            share_out.at[step],
-            share_in.at[z],
-            share_send.at[step],
-            share_recv.at[z],
-            {"hist": src},
-        )
-        copy.start()
-        sends.append(copy)
+        block = block_at(step)
+        for chunk in range(chunks):
+            arrive(block, chunk)
+            if chunk == 0:
+                live = live_of(block)
+            for i in range(per_chunk):
+                cols = slice(i * DH, (i + 1) * DH)
+                share_out[step, chunk, :, cols] = attend(
+                    q_all[block, chunk, :, cols], live, chunk * per_chunk + i
+                )
+            copy = share_copy(step, chunk)
+            copy.start()
+            sends.append(copy)
 
     for step in range(1, n_hist):
-        src = partner_of(z, step, n_hist)
-        remote(
-            share_out.at[step], share_in.at[src], share_send.at[step], share_recv.at[src], {"hist": src}
-        ).wait_recv()
-    attended = share_in[0].astype(F32)
-    for s in range(1, n_hist):
-        attended = attended + share_in[s].astype(F32)
+        src = block_at(step)
+        for chunk in range(chunks):
+            remote(
+                share_out.at[step, chunk],
+                share_in.at[src, chunk],
+                share_send.at[step, chunk],
+                share_recv.at[src, chunk],
+                {"hist": src},
+            ).wait_recv()
+    parts = []
+    for chunk in range(chunks):
+        part = share_in[0, chunk].astype(F32)
+        for s in range(1, n_hist):
+            part = part + share_in[s, chunk].astype(F32)
+        parts.append(part)
+    attended = jnp.concatenate(parts, axis=1)
 
     row_sum = jnp.sum(attended, axis=1, keepdims=True)
     row_squares = jnp.sum(attended * attended, axis=1, keepdims=True)
@@ -319,6 +405,18 @@
     for copy in sends:
         copy.wait_send()
 
+    def sent(distance, there, back, behind):
+        user_copy(there).wait_send()
+        for chunk in range(chunks):
+            query_copy(there, chunk).wait_send()
+
+    each_other(sent)
+
+
+def hand_over(states_in, scores_in, states_out, scores_out):
+    states_out[...] = states_in[...]
+    scores_out[...] = scores_in[...]
+
 
 def local(
     queries,
@@ -338,6 +436,7 @@
 ):
     rows, feat = queries.shape
     hidden = tower_in.shape[1] // 2
+    chunks = CHUNKS if (feat // DH) % CHUNKS == 0 else 1
     any_spec = pl.BlockSpec(memory_space=pl.ANY)
     vmem_spec = pl.BlockSpec(memory_space=pltpu.VMEM)
     dma = pltpu.SemaphoreType.DMA
@@ -350,29 +449,31 @@
         in_specs=[any_spec] * 5 + [pl.BlockSpec(memory_space=pltpu.SMEM)] + [any_spec] * 5,
         out_specs=(vmem_spec, vmem_spec),
         scratch_shapes=[
-            pltpu.VMEM((n_hist, rows, feat), BF16),
+            pltpu.VMEM((rows, feat), BF16),
+            pltpu.VMEM((n_hist, chunks, rows, feat // chunks), BF16),
             pltpu.VMEM((n_hist, 1, rows), jnp.int32),
             pltpu.VMEM(hist_keys.shape, BF16),
             pltpu.VMEM(hist_values.shape, BF16),
             pltpu.VMEM(time_bucket.shape, jnp.int32),
             pltpu.VMEM((rows, feat), BF16),
-            pltpu.VMEM(time_bias.shape, F32),
+            pltpu.VMEM(time_bias.shape[::-1], F32),
             pltpu.VMEM((2, feat, hidden), BF16),
             pltpu.VMEM((1, hidden), F32),
             pltpu.VMEM((1, hidden), F32),
-            pltpu.VMEM((n_hist, rows, feat), BF16),
-            pltpu.VMEM((n_hist, rows, feat), BF16),
+            pltpu.VMEM((n_hist, chunks, rows, feat // chunks), BF16),
+            pltpu.VMEM((n_hist, chunks, rows, feat // chunks), BF16),
             pltpu.VMEM((2, rows, 128), F32),
             pltpu.VMEM((n_tower, 2, rows, feat), BF16),
             pltpu.VMEM((n_tower, 8, rows), F32),
             pltpu.VMEM((n_tower, 2, 8, rows), F32),
             dma((10,)),
+            pltpu.SemaphoreType.REGULAR((n_hist,)),
+            dma((n_hist, chunks)),
+            dma((n_hist, chunks)),
             dma((n_hist,)),
             dma((n_hist,)),
-            dma((n_hist,)),
-            dma((n_hist,)),
-            dma((n_hist,)),
-            dma((n_hist,)),
+            dma((n_hist, chunks)),
+            dma((n_hist, chunks)),
             dma((2,)),
             dma((2,)),
             dma((2 * n_tower,)),
@@ -389,11 +490,20 @@
         time_bucket,
         hist_len,
         cand_gate,
-        time_bias,
+        time_bias.T,
         tower_in,
         tower_bias.reshape(1, -1),
         tower_out.reshape(1, -1),
     )
+    states, scores = pl.pallas_call(
+        hand_over,
+        out_shape=(
+            jax.ShapeDtypeStruct((rows, feat), BF16),
+            jax.ShapeDtypeStruct((1, rows), F32),
+        ),
+        in_specs=[vmem_spec, vmem_spec],
+        out_specs=(vmem_spec, vmem_spec),
+    )(states, scores)
     return states, scores.reshape(rows)
 
 

time: 34 us -> 31.3 us (0.921)
  local copies, waits for them, and re-layouts: 4.01 us -> 0 us
  Pallas kernels: 29.1 us -> 30.5 us
    unnamed x3 -> x0, local copies, waits for them, and re-layouts: 4.01 us -> none
    pallas_call x0 -> x1, Pallas kernels: none -> 1.48 us  [local(): pl.pallas_call(hand_over, out_shape=(jax.ShapeDtypeStruct((rows, feat), B...]
where the time goes in v2:
time: 31.3 us; the launch traced here: 31.2 us
  Pallas kernels  30.5 us (97%)
  between operations  0.64 us (2%)
    pallas_call x1, Pallas kernels, local(): pl.pallas_call(functools.partial(kernel, n_hist, n_tower), out_shape=(jax...  29 us
    pallas_call x1, Pallas kernels, local(): pl.pallas_call(hand_over, out_shape=(jax.ShapeDtypeStruct((rows, feat), B...  1.48 us

profile of v2, /device:TPU:0, one launch (start us, length us, event | category | flops | bytes accessed | tf_op | source)
XLA Modules:
  0.0 31.2 jit_solution(12256896765754861007)
XLA Ops:
  0.6 29.0 %shard_map.122 = (bf16[64,512]{1,0:T(8,128)(2,1)}, f32[1,64]{1,0:T(1,128)}) custom-call(bf16[64,512]{1,0:T(8,128)(2,1)} %q_hbm.1, bf16[2,256,512]{2,1,0:T(8,128)(2,1)} %k_hbm.1, bf16[2,256,512]{2,1,0:T(8,128)(2,1)} %v_hbm.1, s32[1,64]{1,0:T(1,128)} %bitcast.8, s32[2,256]{1,0:T(2,128)} %bucket_hbm.1, s32[2]{0:T(128)} %len_ref.1, bf16[64,512]{1,0:T(8,128)(2,1)} %gate_hbm.1, ...), custom_call_target="tpu_custom_call" | custom-call | tf_op jit(solution)/shard_map/pallas_call | solution.py:443
  29.7 1.5 %shard_map.123 = (bf16[64,512]{1,0:T(8,128)(2,1)}, f32[1,64]{1,0:T(1,128)}) custom-call(bf16[64,512]{1,0:T(8,128)(2,1)} %get-tuple-element.6.states_in, f32[1,64]{1,0:T(1,128)} %get-tuple-element.7.scores_in), custom_call_target="tpu_custom_call" | custom-call | tf_op jit(solution)/shard_map/pallas_call | solution.py:498

commit v3 on v2

--- a/solution.py
+++ b/solution.py
@@ -66,6 +66,7 @@
     score_in,
     load_sem,
     ready,
+    pass_send,
     q_send,
     q_recv,
     u_send,
@@ -164,6 +165,23 @@
                     functools.partial(action, distance, there, z - sign, behind)
                 )
 
+    def goes_direct(distance, behind):
+        return jnp.logical_not(behind) if distance == 2 else z >= 0
+
+    passes = (
+        ((z >= 2) & (z + 1 < n_hist), z - 1, z + 1),
+        ((z >= 1) & (z + 2 < n_hist), z + 1, z - 1),
+    )
+
+    def pass_copy(way, block, there, chunk):
+        return remote(
+            q_all.at[block, chunk],
+            q_all.at[block, chunk],
+            pass_send.at[way, chunk],
+            q_recv.at[block, chunk],
+            {"hist": there},
+        )
+
     def send_queries(distance, there, back, behind):
         if distance > 1:
             pl.semaphore_wait(ready.at[there], 1)
@@ -175,8 +193,11 @@
             )
 
         user_copy(there).start()
-        for chunk in range(chunks):
-            query_copy(there, chunk).start()
+
+        @pl.when(goes_direct(distance, behind))
+        def _():
+            for chunk in range(chunks):
+                query_copy(there, chunk).start()
 
     each_other(send_queries)
     sends = []
@@ -252,11 +273,12 @@
         rest = jnp.where(z < n_hist - 1 - z, z + step - nearer, z - step + nearer)
         return jnp.where(step <= 2 * nearer, paired, rest)
 
+    def users_arrive(block):
+        remote(
+            user_hbm, u_all.at[block], u_send.at[block], u_recv.at[block], {"hist": block}
+        ).wait_recv()
+
     def arrive(block, chunk):
-        if chunk == 0:
-            remote(
-                user_hbm, u_all.at[block], u_send.at[block], u_recv.at[block], {"hist": block}
-            ).wait_recv()
         remote(
             q_hbm.at[:, 0:width],
             q_all.at[block, chunk],
@@ -274,10 +296,25 @@
             {"hist": block_at(step)},
         )
 
+    for chunk in range(chunks):
+        for way, (passing, block, there) in enumerate(passes):
+
+            @pl.when(passing)
+            def _(way=way, block=block, there=there, chunk=chunk):
+                arrive(block, chunk)
+                pass_copy(way, block, there, chunk).start()
+
     for step in range(1, n_hist):
         block = block_at(step)
+        taken = (passes[0][0] & (block == z - 1)) | (passes[1][0] & (block == z + 1))
         for chunk in range(chunks):
-            arrive(block, chunk)
+            if chunk == 0:
+                users_arrive(block)
+
+            @pl.when(jnp.logical_not(taken))
+            def _(block=block, chunk=chunk):
+                arrive(block, chunk)
+
             if chunk == 0:
                 live = live_of(block)
             for i in range(per_chunk):
@@ -407,10 +444,19 @@
 
     def sent(distance, there, back, behind):
         user_copy(there).wait_send()
-        for chunk in range(chunks):
-            query_copy(there, chunk).wait_send()
+
+        @pl.when(goes_direct(distance, behind))
+        def _():
+            for chunk in range(chunks):
+                query_copy(there, chunk).wait_send()
 
     each_other(sent)
+    for way, (passing, block, there) in enumerate(passes):
+
+        @pl.when(passing)
+        def _(way=way, block=block, there=there):
+            for chunk in range(chunks):
+                pass_copy(way, block, there, chunk).wait_send()
 
 
 def hand_over(states_in, scores_in, states_out, scores_out):
@@ -468,6 +514,7 @@
             pltpu.VMEM((n_tower, 2, 8, rows), F32),
             dma((10,)),
             pltpu.SemaphoreType.REGULAR((n_hist,)),
+            dma((2, chunks)),
             dma((n_hist, chunks)),
             dma((n_hist, chunks)),
             dma((n_hist,)),

time: 31.3 us -> 30.9 us (0.987)
  Pallas kernels: 30.5 us -> 30.1 us
    pallas_call x1, Pallas kernels: 29 us -> 28.6 us  [local(): pl.pallas_call(functools.partial(kernel, n_hist, n_tower), out_shape=(jax...]
where the time goes in v3:
time: 30.9 us; the launch traced here: 30.7 us
  Pallas kernels  30.1 us (97%)
  between operations  0.64 us (2%)
    pallas_call x1, Pallas kernels, local(): pl.pallas_call(functools.partial(kernel, n_hist, n_tower), out_shape=(jax...  28.6 us
    pallas_call x1, Pallas kernels, local(): pl.pallas_call(hand_over, out_shape=(jax.ShapeDtypeStruct((rows, feat), B...  1.48 us

profile of v3, /device:TPU:0, one launch (start us, length us, event | category | flops | bytes accessed | tf_op | source)
XLA Modules:
  0.0 30.7 jit_solution(6041263637141794632)
XLA Ops:
  0.6 28.6 %shard_map.122 = (bf16[64,512]{1,0:T(8,128)(2,1)}, f32[1,64]{1,0:T(1,128)}) custom-call(bf16[64,512]{1,0:T(8,128)(2,1)} %q_hbm.1, bf16[2,256,512]{2,1,0:T(8,128)(2,1)} %k_hbm.1, bf16[2,256,512]{2,1,0:T(8,128)(2,1)} %v_hbm.1, s32[1,64]{1,0:T(1,128)} %bitcast.8, s32[2,256]{1,0:T(2,128)} %bucket_hbm.1, s32[2]{0:T(128)} %len_ref.1, bf16[64,512]{1,0:T(8,128)(2,1)} %gate_hbm.1, ...), custom_call_target="tpu_custom_call" | custom-call | tf_op jit(solution)/shard_map/pallas_call | solution.py:489
  29.3 1.5 %shard_map.123 = (bf16[64,512]{1,0:T(8,128)(2,1)}, f32[1,64]{1,0:T(1,128)}) custom-call(bf16[64,512]{1,0:T(8,128)(2,1)} %get-tuple-element.6.states_in, f32[1,64]{1,0:T(1,128)} %get-tuple-element.7.scores_in), custom_call_target="tpu_custom_call" | custom-call | tf_op jit(solution)/shard_map/pallas_call | solution.py:545
